TPU v7x, 1024 devices: a whole 4x4x32 slice. The times are simulated.
1024 devices in a mesh: segment: 2 (over y_hi), fsdp: 32 (over z), seq: 16 (over y_lo, x, core).
Axes of the slice: x: 4, y: 4 (y_hi: 2, y_lo: 2; y = y_hi * 2 + y_lo), z: 32, core: 2. Of those that a mesh axis runs over, the one named last changes fastest.
Arguments:
- branch_x: bfloat16 [64, 2048, 4096], P(('segment', 'fsdp'), 'seq'), may hold values from -6 to 6
- positions: int32 [64, 2048], P(('segment', 'fsdp'), 'seq'), may hold values from 0 to 2047, as said below
- teacher_held: bfloat16 [64, 2048, 4096], P(('segment', 'fsdp'), 'seq'), may hold values from -6 to 6
- gate_weights: bfloat16 [32, 2, 128, 128], P('fsdp'), may hold values from -0.5 to 0.5
- gate_bias: float32 [2, 4096], replicated, may hold values from -4 to 4
- conv_weight: float32 [4, 4096], replicated, may hold values from -3 to 3
- conv_bias: float32 [4096], replicated, may hold values from -3 to 3
- decay_rate: float32 [4096], replicated, as said below
Outputs:
- student_out: bfloat16 [64, 2048, 4096], P(('segment', 'fsdp'), 'seq')
- token_loss: float32 [64, 2048], P(('segment', 'fsdp'), 'seq')
Inputs may be any that keep to these rules, and one draw needn't show every extreme that they name: `positions`: within each sequence a token's position is 0 at a document start and one more than the previous token's position otherwise; every sequence begins with a document start; the first sequence is one whole document. `decay_rate`: rates are positive.
All inputs are finite; a program needn't handle non-finite values.
Results may differ from a plain program's by a relative error of at most 0.0055.
Values may be sent and summed in bfloat16 or wider, within the bound.
A program may use at most 64 MiB of HBM per device.

v0:
```python
import jax
import jax.numpy as jnp
from jax import lax
from jax.sharding import PartitionSpec as P

HEADS = 32
HS = 128


def prefix(value, axis, combine, identity):
    devices, here = (lax.axis_size(axis), lax.axis_index(axis))
    everything = jax.tree.map(lambda part: lax.all_gather(part, axis), value)
    start = jax.tree.map(
        lambda part, zero: jnp.broadcast_to(jnp.asarray(zero, part.dtype), part.shape),
        value,
        identity,
    )

    def hop(k, before):
        reached = k < here
        new = combine(before, jax.tree.map(lambda part: part[k], everything))
        return jax.tree.map(lambda a, b: jnp.where(reached, a, b), new, before)

    return lax.fori_loop(0, devices, hop, start)


def from_partner(value, axis, apart):
    return lax.ppermute(value, axis, [(i, i ^ 1 << apart) for i in range(lax.axis_size(axis))])


def from_behind(value, axis, steps):
    count = lax.axis_size(axis)
    leading, last = (max(0, -steps), min(count, count - steps))
    return lax.ppermute(value, axis, [(source, source + steps) for source in range(leading, last)])


def combine(former, latter):
    return (former[0] * latter[0], latter[0] * former[1] + latter[1])


def recurrence(conv_rows, gate_pre_x, gate_pre_a, bias_pair, rates, places):
    group = conv_rows.shape[0]
    tokens = conv_rows.shape[1]
    width = conv_rows.shape[2]
    blocks = tokens // 8
    seq_total = lax.axis_size("seq") * tokens
    gate_x = jax.nn.sigmoid(gate_pre_x + bias_pair[0])
    gate_a = jax.nn.sigmoid(gate_pre_a + bias_pair[1])
    log_a = -8.0 * gate_a * rates / seq_total
    reset = (places == 0)[:, :, None]
    decay = jnp.where(reset, jnp.float32(0.0), jnp.exp(log_a))
    scale = jnp.where(reset, jnp.float32(1.0), jnp.sqrt(-jnp.expm1(2.0 * log_a)))
    drive = conv_rows.astype(jnp.float32) * gate_x * scale
    decay_blocks = decay.reshape(group, blocks, 8, width)
    drive_blocks = drive.reshape(group, blocks, 8, width)
    running_prod = jnp.ones((group, blocks, width), jnp.float32)
    running_state = jnp.zeros((group, blocks, width), jnp.float32)
    prod_list = []
    state_list = []
    for inner in range(8):
        step_decay = decay_blocks[:, :, inner, :]
        running_prod = running_prod * step_decay
        running_state = step_decay * running_state + drive_blocks[:, :, inner, :]
        prod_list.append(running_prod)
        state_list.append(running_state)
    block_prod = jnp.swapaxes(running_prod, 0, 1)
    block_state = jnp.swapaxes(running_state, 0, 1)

    def across(carry, pair):
        after = combine(carry, pair)
        return (after, carry)

    start = (jnp.ones((group, width), jnp.float32), jnp.zeros((group, width), jnp.float32))
    ending, befores = lax.scan(across, start, (block_prod, block_state))
    identity = (jnp.ones_like(ending[0]), jnp.zeros_like(ending[1]))
    incoming = prefix(ending, "seq", combine, identity)
    entering = befores[1] + befores[0] * incoming[1][None, :, :]
    entering = jnp.swapaxes(entering, 0, 1)[:, :, None, :]
    products = jnp.stack(prod_list, axis=2)
    local_state = jnp.stack(state_list, axis=2)
    full = local_state + products * entering
    return full.reshape(group, tokens, width).astype(jnp.bfloat16)


def local(
    branch_x, positions, teacher_held, gate_weights, gate_bias, conv_weight, conv_bias, decay_rate
):
    tokens = branch_x.shape[1]
    width = branch_x.shape[2]
    target = from_partner(teacher_held, "segment", 0)
    previous = from_behind(branch_x[:, -3:, :], "seq", 1)
    extended = jnp.concatenate([previous, branch_x], axis=1).astype(jnp.float32)
    conv = jnp.zeros((1, tokens, width), jnp.float32) + conv_bias
    for lag_steps in range(4):
        valid = (positions >= lag_steps).astype(jnp.float32)[:, :, None]
        conv = (
            conv
            + conv_weight[lag_steps]
            * extended[:, 3 - lag_steps : 3 - lag_steps + tokens, :]
            * valid
        )
    conv_rounded = conv.astype(jnp.bfloat16)
    by_heads = conv_rounded.reshape(1, tokens, HEADS, HS)
    preact = jnp.einsum(
        "nthi,hgij->ngthj",
        by_heads,
        lax.all_gather(gate_weights, "fsdp", axis=0, tiled=True),
        preferred_element_type=jnp.float32,
    )
    student = recurrence(
        conv_rounded,
        preact[:, 0].reshape(1, tokens, width),
        preact[:, 1].reshape(1, tokens, width),
        gate_bias,
        decay_rate,
        positions,
    )
    student_f = student.astype(jnp.float32)
    normed = student_f * lax.rsqrt(jnp.mean(student_f * student_f, axis=-1, keepdims=True) + 1e-06)
    token_loss = jnp.mean((normed - target.astype(jnp.float32)) ** 2, axis=-1)
    return (student, token_loss)


def solution(mesh):
    in_specs = (
        P(("segment", "fsdp"), "seq", None),
        P(("segment", "fsdp"), "seq"),
        P(("segment", "fsdp"), "seq", None),
        P("fsdp", None, None, None),
        P(),
        P(),
        P(),
        P(),
    )
    out_specs = (P(("segment", "fsdp"), "seq", None), P(("segment", "fsdp"), "seq"))
    return jax.shard_map(local, mesh=mesh, in_specs=in_specs, out_specs=out_specs, check_vma=False)
```

profile of v0, /device:TPU:25, one launch (start us, length us, event | category | flops | bytes accessed | tf_op | source)
XLA Modules:
  0.0 284.5 jit_solution(4086245502598592292)
XLA Ops:
  7.2 0.7 all-gather.6.cloned.1.call-update
  7.9 0.9 slice.90
  8.8 3.7 %collective-permute-start = (bf16[1,3,4096]{2,1,0:T(4,128)(2,1)S(1)}, bf16[1,3,4096]{2,1,0:T(4,128)(2,1)S(1)}, u32[]{:S(2)}, u32[]{:S(2)}) collective-permute-start(bf16[1,3,4096]{2,1,0:T(4,128)(2,1)S(1)} %slice.90), channel_id=1, source_target_pairs={{0,1},{1,2},{2,3},{3,4},{4,5},{5,6},{6,7},{7,8},{8,9},{9,10},{10,1... | collective-permute-start | bytes 73736 | tf_op jit(solution)/shard_map/ppermute | solution.py:34
  12.5 2.9 %collective-permute-start.1 = (bf16[1,128,4096]{2,1,0:T(8,128)(2,1)}, bf16[1,128,4096]{2,1,0:T(8,128)(2,1)}, u32[]{:S(2)}, u32[]{:S(2)}) collective-permute-start(bf16[1,128,4096]{2,1,0:T(8,128)(2,1)} %param.14), channel_id=1, source_target_pairs={{0,512},{512,0},{1,513},{513,1},{2,514},{514,2},{3,515},{515,3},{4... | collective-permute-start | bytes 3145736 | tf_op jit(solution)/shard_map/ppermute | solution.py:28
  15.3 0.7 broadcast_multiply_fusion
  16.1 0.9 fusion.43
  16.9 1.1 fusion.42
  18.0 0.7 compare_reduce_fusion
  18.8 1.5 maximum_convert_fusion
  20.3 1.4 fusion.45
  22.0 115.2 %all-gather.6.cloned.1.call-done = bf16[32,2,128,128]{3,2,1,0:T(8,128)(2,1)} async-done(((bf16[1,2,128,128]{3,2,1,0:T(8,128)(2,1)}), bf16[32,2,128,128]{3,2,1,0:T(8,128)(2,1)}) %all-gather.6.cloned.1.call-update) | async-done | bytes 2097168 | tf_op jit(solution)/shard_map/all_gather | solution.py:107
  137.1 4.1 %copy.30 = bf16[32,2,128,128]{2,3,1,0:T(8,128)(2,1)} copy(bf16[32,2,128,128]{3,2,1,0:T(8,128)(2,1)} %all-gather.6.cloned.1.call-done) | data formatting | bytes 4194304 | tf_op jit(solution)/shard_map/all_gather | solution.py:107
  141.2 2.3 fusion.11
  143.5 2.3 fusion.41
  145.8 3.1 %copy.31 = f32[1,1,128,32,128]{4,3,0,2,1:T(8,128)} copy(f32[1,1,128,32,128]{2,4,1,3,0:T(8,128)} %get-tuple-element.229) | data formatting | bytes 4194304 | tf_op jit(solution)/shard_map/slice | solution.py:113
  148.9 7.7 %broadcast_select_fusion.4 = f32[1,16,8,4096]{3,0,2,1:T(1,128)S(1)} fusion(pred[16,8]{1,0:T(8,128)(4,1)S(1)} %broadcast_in_dim.42, f32[1,16,8,4096]{3,0,2,1:T(1,128)} %bitcast.234, f32[4096]{0:T(1024)S(1)} %broadcast_multiply_fusion, f32[4096]{0:T(1024)S(1)} %bitcast.242), kind=kLoop, calls=%fused_computation.11 | loop fusion | flops 3670016 | bytes 4227200 | tf_op jit(solution)/shard_map/jit(_where)/select_n | solution.py:51
  156.6 2.2 fusion.13
  158.9 3.2 %bitcast_multiply_fusion.29 = (f32[1,16,1,4096]{3,2,1,0:T(1,128)}, f32[1,16,1,4096]{3,2,1,0:T(1,128)}, f32[1,16,1,4096]{3,2,1,0:T(1,128)}, f32[1,16,1,4096]{3,2,...) fusion(f32[1,16,8,4096]{3,0,2,1:T(1,128)S(1)} %broadcast_select_fusion.4), kind=kLoop, calls=%fused_computation.77 | loop fusion | flops 458752 | bytes 3932160 | tf_op jit(solution)/shard_map/mul | solution.py:62
  162.0 2.9 %copy.34 = f32[1,128,4096]{2,1,0:T(8,128)} copy(f32[1,128,4096]{1,2,0:T(8,128)} %bitcast.231) | data formatting | bytes 4194304 | tf_op jit(solution)/shard_map/reshape;squeeze | solution.py:113
  165.0 2.9 %copy.33 = f32[1,128,4096]{2,1,0:T(8,128)} copy(f32[1,128,4096]{1,2,0:T(8,128)} %bitcast.235) | data formatting | bytes 4194304 | tf_op jit(solution)/shard_map/reshape;squeeze | solution.py:112
  167.9 5.2 %multiply_bitcast_fusion = f32[1,16,8,4096]{3,2,1,0:T(8,128)S(1)} fusion(f32[1,128,4096]{2,1,0:T(8,128)} %copy.34, f32[1,128,4096]{2,1,0:T(8,128)} %copy.33, f32[4096]{0:T(1024)S(1)} %broadcast_multiply_fusion, f32[4096]{0:T(1024)S(1)} %bitcast.243, f32[4096]{0:T(1024)S(1)} %bitcast.252, pred[128]{0:T(512)(128)(4,1)S(1)} %get-tuple-element.237, ...), kind=kLoop, calls=%fused_computation.31 | loop fusion | flops 14680064 | bytes 14813312 | tf_op jit(solution)/shard_map/reshape | solution.py:55
  173.1 2.1 fusion.16
  175.7 13.5 %while.31 = (s32[]{:T(128)}, f32[1,4096]{1,0:T(1,128)S(1)}, f32[1,4096]{1,0:T(1,128)S(1)}, f32[16,1,4096]{2,1,0:T(1,128)S(1)}, f32[16,1,4096]{2,1,0:T(1,128)S(1)...) while((s32[]{:T(128)}, f32[1,4096]{1,0:T(1,128)S(1)}, ...), condition=%wide.region_1.2_spmd.clone, body=%wide.region_0.1_spmd.clone.sunk | while | flops 28675 | bytes 163952 | solution.py:74
  175.7 0.8 bitcast_add_fusion.3
  176.6 0.8 bitcast_add_fusion.3
  177.4 0.8 bitcast_add_fusion.3
  178.2 0.8 bitcast_add_fusion.3
  179.1 0.8 bitcast_add_fusion.3
  179.9 0.8 bitcast_add_fusion.3
  180.8 0.8 bitcast_add_fusion.3
  181.6 0.8 bitcast_add_fusion.3
  182.5 0.8 bitcast_add_fusion.3
  183.3 0.8 bitcast_add_fusion.3
  184.2 0.8 bitcast_add_fusion.3
  185.0 0.8 bitcast_add_fusion.3
  185.8 0.8 bitcast_add_fusion.3
  186.7 0.8 bitcast_add_fusion.3
  187.5 0.8 bitcast_add_fusion.3
  188.4 0.8 bitcast_add_fusion.3
  189.2 39.9 %all-gather.2 = f32[16,1,4096]{2,1,0:T(1,128)S(1)} all-gather(f32[1,1,4096]{2,1,0:T(1,128)S(1)} %bitcast.239), channel_id=2, replica_groups=mesh['segment'=2,'fsdp'=32,'seq'=16] {'seq'}, dimensions={0}, use_global_device_ids=true | all-gather | bytes 278528 | tf_op jit(solution)/shard_map/all_gather | solution.py:12
  229.0 17.0 %all-gather.3 = f32[16,1,4096]{2,1,0:T(1,128)S(1)} all-gather(f32[1,1,4096]{2,1,0:T(1,128)S(1)} %bitcast.240), channel_id=3, replica_groups=mesh['segment'=2,'fsdp'=32,'seq'=16] {'seq'}, dimensions={0}, use_global_device_ids=true | all-gather | bytes 278528 | tf_op jit(solution)/shard_map/all_gather | solution.py:12
  246.0 1.0 while.32
  247.5 6.7 %stack.10 = f32[1,16,8,4096]{3,2,1,0:T(8,128)} concatenate(f32[1,16,1,4096]{3,2,1,0:T(1,128)S(1)} %slice_bitcast_fusion, f32[1,16,1,4096]{3,2,1,0:T(1,128)} %get-tuple-element.223, f32[1,16,1,4096]{3,2,1,0:T(1,128)} %get-tuple-element.222, f32[1,16,1,4096]{3,2,1,0:T(1,128)} %get-tuple-element.221, f32[1,16,1,4096]{3,2,1,0:T(1,128)} %get-tuple-element.220, ...), dimensions={2} | concatenate | bytes 4194304 | tf_op jit(solution)/shard_map/stack | solution.py:79
  254.2 10.9 %fusion.29 = (f32[1,16,1,4096]{3,2,1,0:T(1,128)S(1)}, f32[1,16,1,4096]{3,2,1,0:T(1,128)S(1)}, f32[1,16,1,4096]{3,2,1,0:T(1,128)S(1)}, f32[1,16,1,4096]{3,2,1,0:T...) fusion(f32[1,16,8,4096]{3,2,1,0:T(8,128)} %copy-done.3, ...), kind=kLoop, calls=%fused_computation.79 | loop fusion | flops 1048576 | bytes 6291456 | tf_op jit(solution)/shard_map/add | solution.py:63
  265.1 6.5 %stack.8 = f32[1,16,8,4096]{3,2,1,0:T(8,128)} concatenate(f32[1,16,1,4096]{3,2,1,0:T(1,128)} %get-tuple-element.216, f32[1,16,1,4096]{3,2,1,0:T(1,128)} %get-tuple-element.215, f32[1,16,1,4096]{3,2,1,0:T(1,128)} %get-tuple-element.214, f32[1,16,1,4096]{3,2,1,0:T(1,128)} %get-tuple-element.213, f32[1,16,1,4096]{3,2,1,0:T(1,128)S(1)} %get-tuple-element.212, ...), dimensions={2} | concatenate | bytes 4194304 | tf_op jit(solution)/shard_map/stack | solution.py:80
  271.5 2.0 multiply_reduce_fusion.1
  273.6 3.6 %multiply_reduce_fusion = (f32[128]{0:T(128)S(1)}, bf16[1,128,4096]{2,1,0:T(8,128)(2,1)}) fusion(bf16[1,128,4096]{2,1,0:T(8,128)(2,1)} %collective-permute-done.1, f32[128]{0:T(128)S(1)} %rsqrt.12, f32[16,4096]{1,0:T(8,128)S(1)} %bitcast.238, f32[1,16,8,4096]{3,2,1,0:T(8,128)S(1)} %copy-done.4, f32[1,16,8,4096]{3,2,1,0:T(8,128)} %stack.8), kind=kLoop, calls=%fused_computation.28 | loop fusion | flops 4718464 | bytes 6554624 | tf_op jit(solution)/shard_map/reduce_sum | solution.py:120
  277.2 0.5 multiply_bitcast_fusion.1
  (59 shorter events, 2.7 us)
Async XLA Ops:
  7.2 13.2 %copy-start.5 = (f32[4096]{0:T(1024)S(1)}, f32[4096]{0:T(1024)}, u32[]{:S(2)}) copy-start(f32[4096]{0:T(1024)} %param.18) | copy-start | bytes 49156
  7.2 130.0 %all-gather.6.cloned.1.call-start = ((), (), s32[]{:S(2)}) async-start(), calls=%async_computation | async-start | bytes 2162688 | tf_op jit(solution)/shard_map/all_gather | solution.py:107
  8.8 10.0 %collective-permute-start = (bf16[1,3,4096]{2,1,0:T(4,128)(2,1)S(1)}, bf16[1,3,4096]{2,1,0:T(4,128)(2,1)S(1)}, u32[]{:S(2)}, u32[]{:S(2)}) collective-permute-start(bf16[1,3,4096]{2,1,0:T(4,128)(2,1)S(1)} %slice.90), channel_id=1, source_target_pairs={{0,1},{1,2},{2,3},{3,4},{4,5},{5,6},{6,7},{7,8},{8,9},{9,10},{10,1... | collective-permute-start | bytes 73736 | tf_op jit(solution)/shard_map/ppermute | solution.py:34
  12.5 261.1 %collective-permute-start.1 = (bf16[1,128,4096]{2,1,0:T(8,128)(2,1)}, bf16[1,128,4096]{2,1,0:T(8,128)(2,1)}, u32[]{:S(2)}, u32[]{:S(2)}) collective-permute-start(bf16[1,128,4096]{2,1,0:T(8,128)(2,1)} %param.14), channel_id=1, source_target_pairs={{0,512},{512,0},{1,513},{513,1},{2,514},{514,2},{3,515},{515,3},{4... | collective-permute-start | bytes 3145736 | tf_op jit(solution)/shard_map/ppermute | solution.py:28
  156.6 5.4 %copy-start = (f32[1,16,8,4096]{3,0,2,1:T(1,128)}, f32[1,16,8,4096]{3,0,2,1:T(1,128)S(1)}, u32[]{:S(2)}) copy-start(f32[1,16,8,4096]{3,0,2,1:T(1,128)S(1)} %broadcast_select_fusion.4) | copy-start | bytes 6291460
  167.9 5.2 %copy-start.1 = (f32[1,16,8,4096]{3,0,2,1:T(1,128)S(1)}, f32[1,16,8,4096]{3,0,2,1:T(1,128)}, u32[]{:S(2)}) copy-start(f32[1,16,8,4096]{3,0,2,1:T(1,128)} %copy-done) | copy-start | bytes 6291460
  173.1 2.1 copy-start.3
  247.5 6.7 %copy-start.2 = (f32[1,16,8,4096]{3,0,2,1:T(1,128)S(1)}, f32[1,16,8,4096]{3,0,2,1:T(1,128)}, u32[]{:S(2)}) copy-start(f32[1,16,8,4096]{3,0,2,1:T(1,128)} %copy-done) | copy-start | bytes 6291460
  265.1 6.5 %copy-start.4 = (f32[1,16,8,4096]{3,2,1,0:T(8,128)S(1)}, f32[1,16,8,4096]{3,2,1,0:T(8,128)}, u32[]{:S(2)}) copy-start(f32[1,16,8,4096]{3,2,1,0:T(8,128)} %stack.10) | copy-start | bytes 6291460
Sparse Core Ops, SparseCore 0:
  10.7 126.4 all-gather.5
where the time goes:
time: 289 us; the launch traced here: 285 us
  waiting for transfers between devices  116 us (40%)
  blocking collectives  56.8 us (20%)
  other arithmetic  55.8 us (19%)
  local copies, waits for them, and re-layouts  32.2 us (11%)
  between operations  14.3 us (5%)
  starting transfers between devices  6.58 us (2%)
    all_gather x1, waiting for transfers between devices, local(): lax.all_gather(gate_weights, 'fsdp', axis=0, tiled=True)  115 us
    all_gather x2, blocking collectives, prefix(): everything = jax.tree.map(lambda part: lax.all_gather(part, axis), value)  56.8 us
    add x2, other arithmetic, recurrence(): running_state = step_decay * running_state + drive_blocks[:, :, inner, :]  13 us
    add x16, other arithmetic, combine(): return (former[0] * latter[0], latter[0] * former[1] + latter[1])  12.5 us
    select_n x1, other arithmetic, recurrence(): decay = jnp.where(reset, jnp.float32(0.0), jnp.exp(log_a))  7.66 us
    another operation x1, local copies, waits for them, and re-layouts, recurrence(): products = jnp.stack(prod_list, axis=2)  6.67 us
    another operation x1, local copies, waits for them, and re-layouts, recurrence(): local_state = jnp.stack(state_list, axis=2)  6.47 us
  transfers between devices with their start and end apart: 3, of which 1 were waited for; matrix products, arithmetic and copies ran while one was open for 30% of the time, Pallas kernels for 0%

commit v1 on v0

v1 whole, which is shorter than its diff:
```python
import functools

import jax
import jax.numpy as jnp
from jax import lax
from jax.experimental import pallas as pl
from jax.experimental.pallas import tpu as pltpu
from jax.sharding import PartitionSpec as P

HS = 128
MESH = pl.DeviceIdType.MESH
F32 = jnp.float32
BF16 = jnp.bfloat16
SIZES = (1, 2, 2, 2, 1)
BATCHES = len(SIZES)


def sigmoid(v):
    return 1.0 / (1.0 + jnp.exp(-v))


def minus_expm1(y, ey):
    series = 1.0 + y * (1 / 2 + y * (1 / 6 + y * (1 / 24 + y * (1 / 120 + y * (1 / 720)))))
    return jnp.where(y > -0.125, -y * series, 1.0 - ey)


def kernel(
    seq_len,
    x_hbm,
    pos_hbm,
    teach_hbm,
    gw_hbm,
    gb_hbm,
    cw_hbm,
    cb_hbm,
    rate_hbm,
    out_hbm,
    loss_ref,
    x_v,
    halo,
    pos_v,
    gb_v,
    cw_v,
    cb_v,
    rate_v,
    tbuf,
    wbuf,
    convb,
    prod_b,
    local_b,
    comp,
    rowc,
    tot,
    ysum,
    inc_b,
    xf,
    masks,
    tmp,
    acc_b,
    student,
    load_sem,
    out_sem,
    far_s,
    far_r,
    near_s,
    near_r,
    x_s,
    x_r,
    chip_s,
    chip_r,
    row_s,
    row_r,
    y_s,
    y_r,
    t_s,
    t_r,
    h_s,
    h_r,
):
    g, z, s = lax.axis_index("segment"), lax.axis_index("fsdp"), lax.axis_index("seq")
    planes, places = lax.axis_size("fsdp"), lax.axis_size("seq")
    row, here = s // 8, s % 8
    xc, core = here // 2, s % 2
    relay = lax.rem(z, 2) == core

    def at_z(dz):
        return (g, lax.rem(z + dz + planes, planes), s)

    def in_row(other):
        return (g, z, row * 8 + other)

    def remote(src, dst, send, recv, to):
        return pltpu.make_async_remote_copy(
            src_ref=src, dst_ref=dst, send_sem=send, recv_sem=recv, device_id=to, device_id_type=MESH
        )

    def await_bytes(ref, sem):
        pltpu.make_async_copy(ref, ref, sem).wait()

    loads = [
        pltpu.make_async_copy(gw_hbm.at[0], wbuf.at[0], load_sem.at[0]),
        pltpu.make_async_copy(x_hbm.at[0], x_v, load_sem.at[1]),
        pltpu.make_async_copy(pos_hbm, pos_v, load_sem.at[2]),
        pltpu.make_async_copy(cw_hbm, cw_v, load_sem.at[3]),
        pltpu.make_async_copy(cb_hbm, cb_v, load_sem.at[4]),
        pltpu.make_async_copy(gb_hbm, gb_v, load_sem.at[5]),
        pltpu.make_async_copy(rate_hbm, rate_v, load_sem.at[6]),
    ]
    for copy in loads:
        copy.start()

    partner = (1 - g, z, s)
    other_core = in_row(here // 2 * 2 + 1 - core)
    greeted = [at_z(4), at_z(-4), at_z(2), at_z(-2), at_z(1), at_z(-1), partner]
    greeted += [in_row(lax.rem(here + d, 8)) for d in range(1, 8)]
    greeted += [(g, z, lax.rem(s + 8, places))]
    greeted += [(g, z, lax.rem(s + 1, places)), (g, z, lax.rem(s + places - 1, places))]
    barrier = pltpu.get_barrier_semaphore()
    for device in greeted:
        pl.semaphore_signal(barrier, inc=1, device_id=device, device_id_type=MESH)
    loads[0].wait()
    pl.semaphore_wait(barrier, len(greeted))

    quarter = pl.ds(pl.multiple_of(xc * 32, 32), 32)

    def first(j, kind):
        return 8 * j + kind * SIZES[j]

    def piece(u, count):
        return wbuf.at[pl.ds(u, count), :, quarter, :]

    def far_copy(j, down):
        source = 8 * (j - 1) + (1 if down and j > 1 else 0)
        target = 8 * j + (1 if down else 0)
        k = j - 1 + (4 if down else 0)
        return remote(piece(source, 1), piece(target, 1), far_s.at[k], far_r.at[k], at_z(-4 if down else 4))

    def send_near(j):
        count = SIZES[j]
        src = piece(first(j, 0), count)
        for kind, dz in ((3, 2), (1, 1), (2, -1)):
            dst = piece(first(j, kind), count)
            remote(src, dst, near_s.at[j], near_r.at[kind, j], at_z(dz)).start()

    def wait_near(j, kind):
        dst = piece(first(j, kind), SIZES[j])
        await_bytes(dst, near_r.at[kind, j])

    def send_x(j, kind):
        src = piece(first(j, kind), SIZES[j])
        for d in (1, 3, 2):
            to = in_row(lax.rem(xc + d, 4) * 2 + core)
            remote(src, src, x_s.at[kind, j], x_r.at[kind, j], to).start()

    def three(j, kind):
        return wbuf.at[pl.ds(first(j, kind), SIZES[j]), :, pl.ds(0, 96), :]

    def chip_copy(j, kind):
        src = wbuf.at[pl.ds(first(j, kind), SIZES[j])]
        return remote(src, src, chip_s.at[kind, j], chip_r.at[kind, j], other_core)

    def both(for_relay, for_other):
        @pl.when(relay)
        def _():
            for_relay()

        @pl.when(jnp.logical_not(relay))
        def _():
            for_other()

    def start_far(j):
        far_copy(j, False).start()
        if j < 4:
            far_copy(j, True).start()

    def step_far(j):
        @pl.when(relay)
        def _():
            far_copy(j, False).wait_recv()
            if j < 4:
                far_copy(j, True).wait_recv()
                start_far(j + 1)
            send_near(j)
            send_x(j, 0)

    def step_near(j):
        def for_relay():
            wait_near(j, 3)
            send_x(j, 3)

        def for_other():
            for kind in (1, 2):
                wait_near(j, kind)
                send_x(j, kind)

        both(for_relay, for_other)

    def step_x(j):
        def for_relay():
            for kind in (0, 3) if j else (3,):
                await_bytes(three(j, kind), x_r.at[kind, j])
                chip_copy(j, kind).start()

        def for_other():
            for kind in (1, 2):
                await_bytes(three(j, kind), x_r.at[kind, j])
                chip_copy(j, kind).start()

        both(for_relay, for_other)

    def step_chip(j):
        def for_relay():
            for kind in (1, 2):
                chip_copy(j, kind).wait_recv()

        def for_other():
            for kind in (0, 3) if j else (3,):
                chip_copy(j, kind).wait_recv()

        both(for_relay, for_other)

    @pl.when(relay)
    def _():
        start_far(1)
        send_near(0)

    halo_copy = remote(x_hbm.at[0, pl.ds(112, 16), :], halo, h_s, h_r, (g, z, lax.rem(s + 1, places)))
    teacher_copy = remote(teach_hbm.at[0], tbuf, t_s, t_r, partner)

    @pl.when(s < places - 1)
    def _():
        halo_copy.start()

    teacher_copy.start()
    for copy in loads[1:]:
        copy.wait()

    pos = jnp.transpose(jnp.broadcast_to(pos_v[...].astype(F32), (HS, HS)))
    tmp[...] = pos
    for v in range(16):
        places_v = tmp[pl.ds(v, 8, stride=16), :]
        for k in range(3):
            masks[k, pl.ds(8 * v, 8), :] = (places_v >= k + 1.0).astype(F32)
    comp[...] = jnp.zeros_like(comp)
    acc_b[...] = jnp.zeros_like(acc_b)

    def columns(head):
        return pl.ds(pl.multiple_of(head * HS, HS), HS)

    @pl.when(s > 0)
    def _():
        halo_copy.wait_recv()

    @pl.when(s == 0)
    def _():
        halo[...] = jnp.zeros_like(halo)

    def conv_head(head, _):
        cols = columns(head)
        xf[pl.ds(0, 16), :] = halo[:, cols].astype(F32)
        xf[pl.ds(16, HS), :] = x_v[:, cols].astype(F32)
        rows = {v: xf[pl.ds(16 + v, 8, stride=16), :] for v in range(-3, 16)}
        taps = [cw_v[pl.ds(k, 1), cols] for k in range(4)]
        bias = cb_v[:, cols]
        out = []
        for v in range(16):
            total = bias + taps[0] * rows[v]
            for k in range(1, 4):
                total = total + taps[k] * rows[v - k] * masks[k - 1, pl.ds(8 * v, 8), :]
            out.append(total)
        convb[head] = jnp.concatenate(out, axis=0).astype(BF16)
        return 0

    def head_of(j, index):
        count = SIZES[j]
        kind, side = index // count, index % count
        ahead = jnp.where(kind == 0, 0, jnp.where(kind == 1, -1, jnp.where(kind == 2, 1, -2)))
        return lax.rem(z + ahead + jnp.where(side == 0, -4 * j, 4 * j) + 2 * planes, planes)

    sub = lax.broadcasted_iota(jnp.int32, (8, HS), 0)

    def gates(j, index, _):
        u = 8 * j + index
        head = head_of(j, index)
        cols = columns(head)
        rows_b = convb[head]
        pre_x = jnp.dot(rows_b, wbuf[u, 0], preferred_element_type=F32)
        pre_a = jnp.dot(rows_b, wbuf[u, 1], preferred_element_type=F32)
        gate_x = sigmoid(pre_x + gb_v[pl.ds(0, 1), cols])
        gate_a = sigmoid(pre_a + gb_v[pl.ds(1, 1), cols])
        log_a = gate_a * (rate_v[:, cols] * (-8.0 / seq_len))
        keep = masks[0]
        decay = jnp.exp(log_a)
        scale = jnp.sqrt(minus_expm1(2.0 * log_a, decay * decay))
        scale = jnp.where(keep > 0.0, scale, 1.0)
        decay = decay * keep
        drive = rows_b.astype(F32) * gate_x * scale
        prods, states = [decay[0:8]], [drive[0:8]]
        for v in range(1, 16):
            step = decay[8 * v : 8 * v + 8]
            prods.append(prods[-1] * step)
            states.append(step * states[-1] + drive[8 * v : 8 * v + 8])
        p, q = prods[-1], states[-1]
        for d in (1, 2, 4):
            inside = sub >= d
            p_before = jnp.where(inside, pltpu.roll(p, d, 0), 1.0)
            q_before = jnp.where(inside, pltpu.roll(q, d, 0), 0.0)
            q = p * q_before + q
            p = p * p_before
        p_in = jnp.where(sub >= 1, pltpu.roll(p, 1, 0), 1.0)
        q_in = jnp.where(sub >= 1, pltpu.roll(q, 1, 0), 0.0)
        comp[0, pl.ds(u, 1), :] = p[7:8]
        comp[1, pl.ds(u, 1), :] = q[7:8]
        for v in range(16):
            prod_b[u, pl.ds(8 * v, 8), :] = prods[v] * p_in
            local_b[u, pl.ds(8 * v, 8), :] = states[v] + prods[v] * q_in
        return 0

    def compute(j, begin, end):
        lax.fori_loop(begin, end, functools.partial(gates, j), 0)

    def mine(j):
        return pl.ds(8 * j, 8)

    def send_row(j):
        rowc[here, :, mine(j), :] = comp[:, mine(j), :]
        src = comp.at[:, mine(j), :]
        for d in range(1, 8):
            to = in_row(lax.rem(here + d, 8))
            remote(src, rowc.at[here, :, mine(j), :], row_s.at[j], row_r.at[j], to).start()

    def seven(j):
        return rowc.at[pl.ds(0, 7), :, mine(j), :]

    def y_copy(j):
        to = (g, z, lax.rem(s + 8, places))
        return remote(tot.at[mine(j)], ysum.at[mine(j)], y_s.at[j], y_r.at[j], to)

    def step_row(j):
        await_bytes(seven(j), row_r.at[j])
        all_p = jnp.zeros((8, HS), F32) + 1.0
        before_p, before_q, all_q = all_p, jnp.zeros((8, HS), F32), jnp.zeros((8, HS), F32)
        for k in range(8):
            a, b = rowc[k, 0, mine(j), :], rowc[k, 1, mine(j), :]
            before_p = jnp.where(k < here, before_p * a, before_p)
            before_q = jnp.where(k < here, a * before_q + b, before_q)
            all_q = a * all_q + b
        tot[mine(j), :] = all_q

        @pl.when(row == 0)
        def _():
            y_copy(j).start()

        inc_b[0, mine(j), :] = before_p
        inc_b[1, mine(j), :] = before_q

    def step_y(j):
        @pl.when(row == 1)
        def _():
            y_copy(j).wait_recv()
            inc_b[1, mine(j), :] = inc_b[0, mine(j), :] * ysum[mine(j), :] + inc_b[1, mine(j), :]

        def finish(index, _):
            u = 8 * j + index
            cols = columns(head_of(j, index))
            entering = inc_b[1, pl.ds(u, 1), :]
            for v in range(16):
                full = local_b[u, pl.ds(8 * v, 8), :] + prod_b[u, pl.ds(8 * v, 8), :] * entering
                tmp[pl.ds(v, 8, stride=16), :] = full
            rounded = tmp[...].astype(BF16)
            student[:, cols] = rounded
            wide = rounded.astype(F32)
            acc_b[...] += wide * wide
            return 0

        lax.fori_loop(0, 4 * SIZES[j], finish, 0)

    heads = x_v.shape[1] // HS
    lax.fori_loop(0, heads // 2, conv_head, 0)
    step_near(0)
    step_far(1)
    lax.fori_loop(heads // 2, heads, conv_head, 0)
    for j in range(BATCHES):
        step_x(j)
        if j + 1 < BATCHES:
            step_near(j + 1)
        if j + 2 < BATCHES:
            step_far(j + 2)
        step_chip(j)
        compute(j, 0, 2 * SIZES[j])
        if j:
            step_row(j - 1)
        compute(j, 2 * SIZES[j], 4 * SIZES[j])
        send_row(j)
        if j:
            step_y(j - 1)
    step_row(BATCHES - 1)
    step_y(BATCHES - 1)

    out_copy = pltpu.make_async_copy(student, out_hbm.at[0], out_sem)
    out_copy.start()
    width = x_v.shape[1]
    mean_sq = jnp.sum(acc_b[...], axis=1, keepdims=True) * (1.0 / width)
    tmp[...] = jnp.broadcast_to(lax.rsqrt(mean_sq + 1e-06), (HS, HS))
    acc_b[...] = jnp.zeros_like(acc_b)
    teacher_copy.wait_recv()

    def loss_head(head, _):
        cols = columns(head)
        diff = student[:, cols].astype(F32) * tmp[...] - tbuf[:, cols].astype(F32)
        acc_b[...] += diff * diff
        return 0

    lax.fori_loop(0, heads, loss_head, 0)
    loss_ref[...] = jnp.sum(jnp.transpose(acc_b[...]), axis=0, keepdims=True) * (1.0 / width)

    teacher_copy.wait_send()

    @pl.when(s < places - 1)
    def _():
        halo_copy.wait_send()

    @pl.when(row == 0)
    def _():
        for j in range(BATCHES):
            y_copy(j).wait_send()

    for j in range(BATCHES):
        await_bytes(seven(j), row_s.at[j])

    def sent_by_relay():
        for j in range(1, BATCHES):
            far_copy(j, False).wait_send()
            if j < 4:
                far_copy(j, True).wait_send()
        for j in range(BATCHES):
            await_bytes(three(j, 0), near_s.at[j])
            for kind in (0, 3) if j else (3,):
                await_bytes(three(j, kind), x_s.at[kind, j])
                chip_copy(j, kind).wait_send()

    def sent_by_other():
        for j in range(BATCHES):
            for kind in (1, 2):
                await_bytes(three(j, kind), x_s.at[kind, j])
                chip_copy(j, kind).wait_send()

    both(sent_by_relay, sent_by_other)
    out_copy.wait()


def local(branch_x, positions, teacher, gate_weights, gate_bias, conv_weight, conv_bias, decay_rate):
    rows, width = branch_x.shape[1:]
    seq_len = rows * lax.axis_size("seq")
    slots = 8 * BATCHES
    dma = pltpu.SemaphoreType.DMA
    out, loss = pl.pallas_call(
        functools.partial(kernel, seq_len),
        out_shape=(
            jax.ShapeDtypeStruct((1, rows, width), BF16),
            jax.ShapeDtypeStruct((1, rows), F32),
        ),
        in_specs=[pl.BlockSpec(memory_space=pltpu.HBM)] * 8,
        out_specs=(pl.BlockSpec(memory_space=pltpu.HBM), pl.BlockSpec(memory_space=pltpu.VMEM)),
        scratch_shapes=[
            pltpu.VMEM((rows, width), BF16),
            pltpu.VMEM((16, width), BF16),
            pltpu.VMEM((1, rows), jnp.int32),
            pltpu.VMEM((2, width), F32),
            pltpu.VMEM((4, width), F32),
            pltpu.VMEM((1, width), F32),
            pltpu.VMEM((1, width), F32),
            pltpu.VMEM((rows, width), BF16),
            pltpu.VMEM((slots, 2, HS, HS), BF16),
            pltpu.VMEM((width // HS, rows, HS), BF16),
            pltpu.VMEM((slots, rows, HS), F32),
            pltpu.VMEM((slots, rows, HS), F32),
            pltpu.VMEM((2, slots, HS), F32),
            pltpu.VMEM((8, 2, slots, HS), F32),
            pltpu.VMEM((slots, HS), F32),
            pltpu.VMEM((slots, HS), F32),
            pltpu.VMEM((2, slots, HS), F32),
            pltpu.VMEM((rows + 16, HS), F32),
            pltpu.VMEM((3, rows, HS), F32),
            pltpu.VMEM((rows, HS), F32),
            pltpu.VMEM((rows, HS), F32),
            pltpu.VMEM((rows, width), BF16),
            dma((7,)),
            dma,
            dma((8,)),
            dma((8,)),
            dma((BATCHES,)),
            dma((4, BATCHES)),
            dma((4, BATCHES)),
            dma((4, BATCHES)),
            dma((4, BATCHES)),
            dma((4, BATCHES)),
            dma((BATCHES,)),
            dma((BATCHES,)),
            dma((BATCHES,)),
            dma((BATCHES,)),
            dma,
            dma,
            dma,
            dma,
        ],
        compiler_params=pltpu.CompilerParams(
            collective_id=0, has_side_effects=True, vmem_limit_bytes=60 << 20
        ),
        name="step",
    )(
        branch_x,
        positions,
        teacher,
        gate_weights,
        gate_bias,
        conv_weight,
        conv_bias.reshape(1, width),
        decay_rate.reshape(1, width),
    )
    return out, loss


def solution(mesh):
    in_specs = (
        P(("segment", "fsdp"), "seq", None),
        P(("segment", "fsdp"), "seq"),
        P(("segment", "fsdp"), "seq", None),
        P("fsdp", None, None, None),
        P(),
        P(),
        P(),
        P(),
    )
    out_specs = (P(("segment", "fsdp"), "seq", None), P(("segment", "fsdp"), "seq"))
    return jax.shard_map(local, mesh=mesh, in_specs=in_specs, out_specs=out_specs, check_vma=False)
```

time: 289 us -> 67.1 us (0.23); the launches traced: 285 us -> 66.9 us
  waiting for transfers between devices: 116 us -> 0 us
  Pallas kernels: 0 us -> 63.4 us
  blocking collectives: 56.8 us -> 0 us
  other arithmetic: 55.8 us -> 0 us
  local copies, waits for them, and re-layouts: 32.2 us -> 2.8 us
  between operations: 14.3 us -> 0.65 us
  starting transfers between devices: 6.58 us -> 0 us
    all_gather x1 -> x0, waiting for transfers between devices: 115 us -> none  [local(): lax.all_gather(gate_weights, 'fsdp', axis=0, tiled=True)]
    pallas_call x0 -> x1, Pallas kernels: none -> 63.4 us  [local(): pl.pallas_call(functools.partial(kernel, seq_len), out_shape=(jax.ShapeDt...]
    all_gather x2 -> x0, blocking collectives: 56.8 us -> none  [prefix(): everything = jax.tree.map(lambda part: lax.all_gather(part, axis), value)]
    add x19 -> x0, other arithmetic: 25.8 us -> none  [the longest x2 13 us: recurrence(): running_state = step_decay * running_state + drive_blocks[:, :, inner, :]]
    another operation x6 -> x0, local copies, waits for them, and re-layouts: 19.4 us -> none  [the longest x1 6.67 us: recurrence(): products = jnp.stack(prod_list, axis=2)]
    select_n x17 -> x0, other arithmetic: 8.36 us -> none  [the longest x1 7.66 us: recurrence(): decay = jnp.where(reset, jnp.float32(0.0), jnp.exp(log_a))]
    slice x5 -> x0, local copies, waits for them, and re-layouts: 8.19 us -> none  [the longest x1 3.12 us: local(): preact[:, 1].reshape(1, tokens, width)]
    ppermute x2 -> x0, starting transfers between devices: 6.55 us -> none  [the longest x1 3.68 us: from_behind(): lax.ppermute(value, axis, [(source, source + steps) for source in range(l...]
  transfers between devices with their start and end apart: 3 -> 0, of which waited for: 1 -> 0; matrix products, arithmetic and copies ran while one was open for 30% -> 0% of each run, Pallas kernels for 0% -> 0%
where the time goes in v1:
time: 67.1 us; the launch traced here: 66.9 us
  Pallas kernels  63.4 us (94%)
  local copies, waits for them, and re-layouts  2.8 us (4%)
    pallas_call x1, Pallas kernels, local(): pl.pallas_call(functools.partial(kernel, seq_len), out_shape=(jax.ShapeDt...  63.4 us
    unnamed x4, local copies, waits for them, and re-layouts  2.8 us

profile of v1, /device:TPU:25, one launch (start us, length us, event | category | flops | bytes accessed | tf_op | source)
XLA Modules:
  0.0 66.9 jit_solution(16944426756548793450)
XLA Ops:
  0.6 63.4 %step.1 = (bf16[1,128,4096]{2,1,0:T(8,128)(2,1)}, f32[1,128]{1,0:T(1,128)}) custom-call(bf16[1,128,4096]{2,1,0:T(8,128)(2,1)} %x_hbm.1, s32[1,128]{1,0:T(1,128)} %pos_hbm.1, bf16[1,128,4096]{2,1,0:T(8,128)(2,1)} %teach_hbm.1, bf16[1,2,128,128]{3,2,1,0:T(8,128)(2,1)} %gw_hbm.1, f32[2,4096]{1,0:T(2,128)} %gb_hbm.1, f32[4,4096]{1,0:T(4,128)} %cw_hbm.1, ...), custom_call_target="tpu_custom_call" | custom-call | tf_op jit(solution)/shard_map/step/pallas_call | solution.py:457
  64.1 0.0 copy-start
  64.1 2.3 %copy.12 = bf16[1,128,4096]{2,1,0:T(8,128)(2,1)} copy(bf16[1,128,4096]{2,1,0:T(8,128)(2,1)} %get-tuple-element.4) | data formatting | bytes 2097152
  66.4 0.0 copy-done
  66.4 0.5 copy.13
Async XLA Ops:
  64.1 2.3 %copy-start = (f32[1,128]{1,0:T(1,128)S(1)}, f32[1,128]{1,0:T(1,128)}, u32[]{:S(2)}) copy-start(f32[1,128]{1,0:T(1,128)} %get-tuple-element.5) | copy-start | bytes 1540

commit v2 on v1

--- a/solution.py
+++ b/solution.py
@@ -13,6 +13,7 @@
 BF16 = jnp.bfloat16
 SIZES = (1, 2, 2, 2, 1)
 BATCHES = len(SIZES)
+LAST = BATCHES - 1
 
 
 def sigmoid(v):
@@ -50,6 +51,7 @@
     local_b,
     comp,
     rowc,
+    allc,
     tot,
     ysum,
     inc_b,
@@ -70,6 +72,8 @@
     chip_r,
     row_s,
     row_r,
+    all_s,
+    all_r,
     y_s,
     y_r,
     t_s,
@@ -111,16 +115,18 @@
 
     partner = (1 - g, z, s)
     other_core = in_row(here // 2 * 2 + 1 - core)
-    greeted = [at_z(4), at_z(-4), at_z(2), at_z(-2), at_z(1), at_z(-1), partner]
-    greeted += [in_row(lax.rem(here + d, 8)) for d in range(1, 8)]
-    greeted += [(g, z, lax.rem(s + 8, places))]
-    greeted += [(g, z, lax.rem(s + 1, places)), (g, z, lax.rem(s + places - 1, places))]
+    greeted = [at_z(dz) for dz in (8, -8, 4, -4)]
+    for dz in (2, -2, 1, -1):
+        for d in range(4):
+            greeted.append(at_z(dz)[:2] + (row * 8 + lax.rem(xc + d, 4) * 2 + core,))
+    greeted += [partner] + [(g, z, lax.rem(s + d, places)) for d in range(1, 16)]
     barrier = pltpu.get_barrier_semaphore()
     for device in greeted:
         pl.semaphore_signal(barrier, inc=1, device_id=device, device_id_type=MESH)
     loads[0].wait()
     pl.semaphore_wait(barrier, len(greeted))
 
+    blocks = [pl.ds(32 * k, 32) for k in range(4)]
     quarter = pl.ds(pl.multiple_of(xc * 32, 32), 32)
 
     def first(j, kind):
@@ -130,17 +136,21 @@
         return wbuf.at[pl.ds(u, count), :, quarter, :]
 
     def far_copy(j, down):
-        source = 8 * (j - 1) + (1 if down and j > 1 else 0)
+        source = (8 * 2 + (1 if down else 0)) if j > 2 else 0
         target = 8 * j + (1 if down else 0)
         k = j - 1 + (4 if down else 0)
-        return remote(piece(source, 1), piece(target, 1), far_s.at[k], far_r.at[k], at_z(-4 if down else 4))
+        dz = 4 if j % 2 else 8
+        return remote(piece(source, 1), piece(target, 1), far_s.at[k], far_r.at[k], at_z(-dz if down else dz))
 
     def send_near(j):
         count = SIZES[j]
         src = piece(first(j, 0), count)
-        for kind, dz in ((3, 2), (1, 1), (2, -1)):
-            dst = piece(first(j, kind), count)
-            remote(src, dst, near_s.at[j], near_r.at[kind, j], at_z(dz)).start()
+        for d in (2, 1, 3, 0) if j == LAST else (0,):
+            place = row * 8 + lax.rem(xc + d, 4) * 2 + core
+            for kind, dz in ((3, 2), (1, 1), (2, -1)):
+                dst = piece(first(j, kind), count)
+                to = (g, lax.rem(z + dz + planes, planes), place)
+                remote(src, dst, near_s.at[j], near_r.at[kind, j], to).start()
 
     def wait_near(j, kind):
         dst = piece(first(j, kind), SIZES[j])
@@ -154,6 +164,12 @@
 
     def three(j, kind):
         return wbuf.at[pl.ds(first(j, kind), SIZES[j]), :, pl.ds(0, 96), :]
+
+    def await_x(j, kind):
+        if j == LAST and kind:
+            await_bytes(wbuf.at[pl.ds(first(j, kind), 1)], near_r.at[kind, j])
+        else:
+            await_bytes(three(j, kind), x_r.at[kind, j])
 
     def chip_copy(j, kind):
         src = wbuf.at[pl.ds(first(j, kind), SIZES[j])]
@@ -179,11 +195,16 @@
             far_copy(j, False).wait_recv()
             if j < 4:
                 far_copy(j, True).wait_recv()
-                start_far(j + 1)
+            if j == 2:
+                start_far(4)
+                start_far(3)
             send_near(j)
             send_x(j, 0)
 
     def step_near(j):
+        if j == LAST:
+            return
+
         def for_relay():
             wait_near(j, 3)
             send_x(j, 3)
@@ -198,12 +219,12 @@
     def step_x(j):
         def for_relay():
             for kind in (0, 3) if j else (3,):
-                await_bytes(three(j, kind), x_r.at[kind, j])
+                await_x(j, kind)
                 chip_copy(j, kind).start()
 
         def for_other():
             for kind in (1, 2):
-                await_bytes(three(j, kind), x_r.at[kind, j])
+                await_x(j, kind)
                 chip_copy(j, kind).start()
 
         both(for_relay, for_other)
@@ -221,17 +242,22 @@
 
     @pl.when(relay)
     def _():
+        start_far(2)
         start_far(1)
         send_near(0)
 
     halo_copy = remote(x_hbm.at[0, pl.ds(112, 16), :], halo, h_s, h_r, (g, z, lax.rem(s + 1, places)))
-    teacher_copy = remote(teach_hbm.at[0], tbuf, t_s, t_r, partner)
+    teacher_copies = [
+        remote(teach_hbm.at[0, block, :], tbuf.at[block, :], t_s.at[k], t_r.at[k], partner)
+        for k, block in enumerate(blocks)
+    ]
 
     @pl.when(s < places - 1)
     def _():
         halo_copy.start()
 
-    teacher_copy.start()
+    for copy in teacher_copies:
+        copy.start()
     for copy in loads[1:]:
         copy.wait()
 
@@ -317,7 +343,7 @@
         return 0
 
     def compute(j, begin, end):
-        lax.fori_loop(begin, end, functools.partial(gates, j), 0)
+        lax.fori_loop(begin, end, functools.partial(gates, j), 0, unroll=4)
 
     def mine(j):
         return pl.ds(8 * j, 8)
@@ -328,6 +354,31 @@
         for d in range(1, 8):
             to = in_row(lax.rem(here + d, 8))
             remote(src, rowc.at[here, :, mine(j), :], row_s.at[j], row_r.at[j], to).start()
+
+    def last_copy(d):
+        mine_last = pl.ds(8 * LAST, 8)
+        to = (g, z, lax.rem(s + d, places))
+        return remote(comp.at[:, mine_last, :], allc.at[s], all_s.at[d - 1], all_r.at[s], to)
+
+    def send_last():
+        for d in range(15, 0, -1):
+
+            @pl.when(s + d < places)
+            def _():
+                last_copy(d).start()
+
+    def step_last():
+        entering = jnp.zeros((8, HS), F32)
+        for k in range(15):
+
+            @pl.when(k < s)
+            def _():
+                pltpu.make_async_copy(allc.at[k], allc.at[k], all_r.at[k]).wait()
+
+        for k in range(15):
+            through = allc[k, 0] * entering + allc[k, 1]
+            entering = jnp.where(k < s, through, entering)
+        inc_b[1, mine(LAST), :] = entering
 
     def seven(j):
         return rowc.at[pl.ds(0, 7), :, mine(j), :]
@@ -360,6 +411,9 @@
             y_copy(j).wait_recv()
             inc_b[1, mine(j), :] = inc_b[0, mine(j), :] * ysum[mine(j), :] + inc_b[1, mine(j), :]
 
+        finish_batch(j)
+
+    def finish_batch(j):
         def finish(index, _):
             u = 8 * j + index
             cols = columns(head_of(j, index))
@@ -373,48 +427,93 @@
             acc_b[...] += wide * wide
             return 0
 
-        lax.fori_loop(0, 4 * SIZES[j], finish, 0)
+        lax.fori_loop(0, 4 * SIZES[j], finish, 0, unroll=4)
+
+    def sent(j):
+        def by_relay():
+            if j:
+                far_copy(j, False).wait_send()
+                if j < 4:
+                    far_copy(j, True).wait_send()
+            await_bytes(wbuf.at[pl.ds(0, 3)] if j == LAST else three(j, 0), near_s.at[j])
+            for kind in (0, 3) if j else (3,):
+                if j < LAST or kind == 0:
+                    await_bytes(three(j, kind), x_s.at[kind, j])
+                chip_copy(j, kind).wait_send()
+
+        def by_other():
+            for kind in (1, 2):
+                if j < LAST:
+                    await_bytes(three(j, kind), x_s.at[kind, j])
+                chip_copy(j, kind).wait_send()
+
+        both(by_relay, by_other)
 
     heads = x_v.shape[1] // HS
-    lax.fori_loop(0, heads // 2, conv_head, 0)
+    lax.fori_loop(0, heads // 2, conv_head, 0, unroll=4)
     step_near(0)
     step_far(1)
-    lax.fori_loop(heads // 2, heads, conv_head, 0)
+    lax.fori_loop(heads // 2, heads, conv_head, 0, unroll=4)
+    step_x(0)
+    step_far(2)
+    step_near(1)
+    step_chip(0)
+    compute(0, 0, 4)
+    send_row(0)
+    step_near(2)
+    step_x(1)
+    step_far(3)
+    step_chip(1)
+    compute(1, 0, 4)
+    step_x(2)
+    step_far(4)
+    step_near(3)
+    compute(1, 4, 8)
+    send_row(1)
+    step_row(0)
+    step_chip(2)
+    compute(2, 0, 4)
+    step_x(3)
+    step_x(4)
+    step_y(0)
+    compute(2, 4, 8)
+    send_row(2)
+    step_row(1)
+    step_chip(3)
+    compute(3, 0, 4)
+    step_y(1)
+    step_row(2)
+    compute(3, 4, 8)
+    send_row(3)
+    step_chip(4)
+    compute(4, 0, 4)
+    send_last()
+    step_y(2)
+    step_row(3)
     for j in range(BATCHES):
-        step_x(j)
-        if j + 1 < BATCHES:
-            step_near(j + 1)
-        if j + 2 < BATCHES:
-            step_far(j + 2)
-        step_chip(j)
-        compute(j, 0, 2 * SIZES[j])
-        if j:
-            step_row(j - 1)
-        compute(j, 2 * SIZES[j], 4 * SIZES[j])
-        send_row(j)
-        if j:
-            step_y(j - 1)
-    step_row(BATCHES - 1)
-    step_y(BATCHES - 1)
+        sent(j)
+    step_y(3)
+    step_last()
+    finish_batch(LAST)
 
     out_copy = pltpu.make_async_copy(student, out_hbm.at[0], out_sem)
     out_copy.start()
     width = x_v.shape[1]
     mean_sq = jnp.sum(acc_b[...], axis=1, keepdims=True) * (1.0 / width)
     tmp[...] = jnp.broadcast_to(lax.rsqrt(mean_sq + 1e-06), (HS, HS))
-    acc_b[...] = jnp.zeros_like(acc_b)
-    teacher_copy.wait_recv()
-
-    def loss_head(head, _):
-        cols = columns(head)
-        diff = student[:, cols].astype(F32) * tmp[...] - tbuf[:, cols].astype(F32)
-        acc_b[...] += diff * diff
-        return 0
-
-    lax.fori_loop(0, heads, loss_head, 0)
+    for k, block in enumerate(blocks):
+        teacher_copies[k].wait_recv()
+
+        def loss_head(head, total):
+            cols = columns(head)
+            diff = student[block, cols].astype(F32) * tmp[block, :] - tbuf[block, cols].astype(F32)
+            return total + diff * diff
+
+        acc_b[block, :] = lax.fori_loop(0, heads, loss_head, jnp.zeros((32, HS), F32), unroll=4)
     loss_ref[...] = jnp.sum(jnp.transpose(acc_b[...]), axis=0, keepdims=True) * (1.0 / width)
 
-    teacher_copy.wait_send()
+    for copy in teacher_copies:
+        copy.wait_send()
 
     @pl.when(s < places - 1)
     def _():
@@ -422,30 +521,17 @@
 
     @pl.when(row == 0)
     def _():
-        for j in range(BATCHES):
+        for j in range(LAST):
             y_copy(j).wait_send()
 
-    for j in range(BATCHES):
+    for j in range(LAST):
         await_bytes(seven(j), row_s.at[j])
-
-    def sent_by_relay():
-        for j in range(1, BATCHES):
-            far_copy(j, False).wait_send()
-            if j < 4:
-                far_copy(j, True).wait_send()
-        for j in range(BATCHES):
-            await_bytes(three(j, 0), near_s.at[j])
-            for kind in (0, 3) if j else (3,):
-                await_bytes(three(j, kind), x_s.at[kind, j])
-                chip_copy(j, kind).wait_send()
-
-    def sent_by_other():
-        for j in range(BATCHES):
-            for kind in (1, 2):
-                await_bytes(three(j, kind), x_s.at[kind, j])
-                chip_copy(j, kind).wait_send()
-
-    both(sent_by_relay, sent_by_other)
+    for d in range(1, 16):
+
+        @pl.when(s + d < places)
+        def _():
+            last_copy(d).wait_send()
+
     out_copy.wait()
 
 
@@ -454,6 +540,17 @@
     seq_len = rows * lax.axis_size("seq")
     slots = 8 * BATCHES
     dma = pltpu.SemaphoreType.DMA
+    operands = (
+        branch_x,
+        positions,
+        teacher,
+        gate_weights,
+        gate_bias,
+        conv_weight,
+        conv_bias.reshape(1, width),
+        decay_rate.reshape(1, width),
+    )
+    operands = [pltpu.with_memory_space_constraint(v, pltpu.HBM) for v in operands]
     out, loss = pl.pallas_call(
         functools.partial(kernel, seq_len),
         out_shape=(
@@ -477,6 +574,7 @@
             pltpu.VMEM((slots, rows, HS), F32),
             pltpu.VMEM((2, slots, HS), F32),
             pltpu.VMEM((8, 2, slots, HS), F32),
+            pltpu.VMEM((16, 2, 8, HS), F32),
             pltpu.VMEM((slots, HS), F32),
             pltpu.VMEM((slots, HS), F32),
             pltpu.VMEM((2, slots, HS), F32),
@@ -497,27 +595,20 @@
             dma((4, BATCHES)),
             dma((BATCHES,)),
             dma((BATCHES,)),
+            dma((15,)),
+            dma((16,)),
             dma((BATCHES,)),
             dma((BATCHES,)),
-            dma,
-            dma,
+            dma((4,)),
+            dma((4,)),
             dma,
             dma,
         ],
         compiler_params=pltpu.CompilerParams(
-            collective_id=0, has_side_effects=True, vmem_limit_bytes=60 << 20
+            collective_id=0, has_side_effects=True, vmem_limit_bytes=40 << 20
         ),
         name="step",
-    )(
-        branch_x,
-        positions,
-        teacher,
-        gate_weights,
-        gate_bias,
-        conv_weight,
-        conv_bias.reshape(1, width),
-        decay_rate.reshape(1, width),
-    )
+    )(*operands)
     return out, loss
 
 

time: 67.1 us -> 63.3 us (0.943)
  Pallas kernels: 63.4 us -> 60.5 us
  local copies, waits for them, and re-layouts: 2.8 us -> 1.48 us
    pallas_call x1, Pallas kernels: 63.4 us -> 60.5 us  [local(): pl.pallas_call(functools.partial(kernel, seq_len), out_shape=(jax.ShapeDt...]
    unnamed x4 -> x2, local copies, waits for them, and re-layouts: 2.8 us -> 1.48 us
where the time goes in v2:
time: 63.3 us; the launch traced here: 62.6 us
  Pallas kernels  60.5 us (96%)
  local copies, waits for them, and re-layouts  1.48 us (2%)
  between operations  0.64 us (1%)
    pallas_call x1, Pallas kernels, local(): pl.pallas_call(functools.partial(kernel, seq_len), out_shape=(jax.ShapeDt...  60.5 us
    unnamed x2, local copies, waits for them, and re-layouts  1.48 us

profile of v2, /device:TPU:25, one launch (start us, length us, event | category | flops | bytes accessed | tf_op | source)
XLA Modules:
  0.0 62.6 jit_solution(15870319750349017759)
XLA Ops:
  0.6 60.5 %step.1 = (bf16[1,128,4096]{2,1,0:T(8,128)(2,1)S(1)}, f32[1,128]{1,0:T(1,128)S(1)}) custom-call(bf16[1,128,4096]{2,1,0:T(8,128)(2,1)} %x_hbm.1, s32[1,128]{1,0:T(1,128)} %pos_hbm.1, bf16[1,128,4096]{2,1,0:T(8,128)(2,1)} %teach_hbm.1, bf16[1,2,128,128]{3,2,1,0:T(8,128)(2,1)} %gw_hbm.1, f32[2,4096]{1,0:T(2,128)} %gb_hbm.1, f32[4,4096]{1,0:T(4,128)} %cw_hbm.1, ...), custom_call_target="tpu_custom_call" | custom-call | tf_op jit(solution)/shard_map/step/pallas_call | solution.py:554
  61.1 1.0 %copy.12 = bf16[1,128,4096]{2,1,0:T(8,128)(2,1)} copy(bf16[1,128,4096]{2,1,0:T(8,128)(2,1)S(1)} %get-tuple-element.4) | data formatting | bytes 2097152
  62.1 0.5 copy.13

commit v3 on v2

--- a/solution.py
+++ b/solution.py
@@ -14,6 +14,7 @@
 SIZES = (1, 2, 2, 2, 1)
 BATCHES = len(SIZES)
 LAST = BATCHES - 1
+DIRECT = 3
 
 
 def sigmoid(v):
@@ -137,7 +138,7 @@
 
     def far_copy(j, down):
         source = (8 * 2 + (1 if down else 0)) if j > 2 else 0
-        target = 8 * j + (1 if down else 0)
+        target = 8 * j + (1 if down and j < 4 else 0)
         k = j - 1 + (4 if down else 0)
         dz = 4 if j % 2 else 8
         return remote(piece(source, 1), piece(target, 1), far_s.at[k], far_r.at[k], at_z(-dz if down else dz))
@@ -184,17 +185,18 @@
         def _():
             for_other()
 
+    def far_copies(j):
+        return [far_copy(j, down) for down in ((False, True) if j < 4 else (True,))]
+
     def start_far(j):
-        far_copy(j, False).start()
-        if j < 4:
-            far_copy(j, True).start()
+        for copy in far_copies(j):
+            copy.start()
 
     def step_far(j):
         @pl.when(relay)
         def _():
-            far_copy(j, False).wait_recv()
-            if j < 4:
-                far_copy(j, True).wait_recv()
+            for copy in far_copies(j):
+                copy.wait_recv()
             if j == 2:
                 start_far(4)
                 start_far(3)
@@ -342,8 +344,8 @@
             local_b[u, pl.ds(8 * v, 8), :] = states[v] + prods[v] * q_in
         return 0
 
-    def compute(j, begin, end):
-        lax.fori_loop(begin, end, functools.partial(gates, j), 0, unroll=4)
+    def compute(j):
+        lax.fori_loop(0, 4 * SIZES[j], functools.partial(gates, j), 0, unroll=4)
 
     def mine(j):
         return pl.ds(8 * j, 8)
@@ -355,30 +357,32 @@
             to = in_row(lax.rem(here + d, 8))
             remote(src, rowc.at[here, :, mine(j), :], row_s.at[j], row_r.at[j], to).start()
 
-    def last_copy(d):
-        mine_last = pl.ds(8 * LAST, 8)
+    def direct_copy(j, d):
+        k = j - DIRECT
         to = (g, z, lax.rem(s + d, places))
-        return remote(comp.at[:, mine_last, :], allc.at[s], all_s.at[d - 1], all_r.at[s], to)
-
-    def send_last():
+        return remote(comp.at[:, mine(j), :], allc.at[k, s], all_s.at[k, d - 1], all_r.at[k, s], to)
+
+    def send_direct(j):
         for d in range(15, 0, -1):
 
             @pl.when(s + d < places)
             def _():
-                last_copy(d).start()
-
-    def step_last():
+                direct_copy(j, d).start()
+
+    def step_direct(j):
+        c = j - DIRECT
+        for k in range(15):
+
+            @pl.when(k < s)
+            def _():
+                pltpu.make_async_copy(allc.at[c, k], allc.at[c, k], all_r.at[c, k]).wait()
+
         entering = jnp.zeros((8, HS), F32)
         for k in range(15):
-
-            @pl.when(k < s)
-            def _():
-                pltpu.make_async_copy(allc.at[k], allc.at[k], all_r.at[k]).wait()
-
-        for k in range(15):
-            through = allc[k, 0] * entering + allc[k, 1]
+            through = allc[c, k, 0] * entering + allc[c, k, 1]
             entering = jnp.where(k < s, through, entering)
-        inc_b[1, mine(LAST), :] = entering
+        inc_b[1, mine(j), :] = entering
+        finish_batch(j)
 
     def seven(j):
         return rowc.at[pl.ds(0, 7), :, mine(j), :]
@@ -432,9 +436,8 @@
     def sent(j):
         def by_relay():
             if j:
-                far_copy(j, False).wait_send()
-                if j < 4:
-                    far_copy(j, True).wait_send()
+                for copy in far_copies(j):
+                    copy.wait_send()
             await_bytes(wbuf.at[pl.ds(0, 3)] if j == LAST else three(j, 0), near_s.at[j])
             for kind in (0, 3) if j else (3,):
                 if j < LAST or kind == 0:
@@ -458,43 +461,38 @@
     step_far(2)
     step_near(1)
     step_chip(0)
-    compute(0, 0, 4)
+    compute(0)
     send_row(0)
     step_near(2)
     step_x(1)
     step_far(3)
     step_chip(1)
-    compute(1, 0, 4)
+    compute(1)
+    send_row(1)
     step_x(2)
     step_far(4)
     step_near(3)
-    compute(1, 4, 8)
-    send_row(1)
     step_row(0)
     step_chip(2)
-    compute(2, 0, 4)
+    compute(2)
+    send_row(2)
     step_x(3)
     step_x(4)
+    step_row(1)
     step_y(0)
-    compute(2, 4, 8)
-    send_row(2)
-    step_row(1)
     step_chip(3)
-    compute(3, 0, 4)
+    compute(3)
+    send_direct(3)
+    step_row(2)
+    step_chip(4)
+    compute(4)
+    send_direct(4)
     step_y(1)
-    step_row(2)
-    compute(3, 4, 8)
-    send_row(3)
-    step_chip(4)
-    compute(4, 0, 4)
-    send_last()
-    step_y(2)
-    step_row(3)
     for j in range(BATCHES):
         sent(j)
-    step_y(3)
-    step_last()
-    finish_batch(LAST)
+    step_y(2)
+    step_direct(3)
+    step_direct(4)
 
     out_copy = pltpu.make_async_copy(student, out_hbm.at[0], out_sem)
     out_copy.start()
@@ -521,16 +519,17 @@
 
     @pl.when(row == 0)
     def _():
-        for j in range(LAST):
+        for j in range(DIRECT):
             y_copy(j).wait_send()
 
-    for j in range(LAST):
+    for j in range(DIRECT):
         await_bytes(seven(j), row_s.at[j])
     for d in range(1, 16):
 
         @pl.when(s + d < places)
         def _():
-            last_copy(d).wait_send()
+            for j in range(DIRECT, BATCHES):
+                direct_copy(j, d).wait_send()
 
     out_copy.wait()
 
@@ -574,7 +573,7 @@
             pltpu.VMEM((slots, rows, HS), F32),
             pltpu.VMEM((2, slots, HS), F32),
             pltpu.VMEM((8, 2, slots, HS), F32),
-            pltpu.VMEM((16, 2, 8, HS), F32),
+            pltpu.VMEM((BATCHES - DIRECT, 16, 2, 8, HS), F32),
             pltpu.VMEM((slots, HS), F32),
             pltpu.VMEM((slots, HS), F32),
             pltpu.VMEM((2, slots, HS), F32),
@@ -595,8 +594,8 @@
             dma((4, BATCHES)),
             dma((BATCHES,)),
             dma((BATCHES,)),
-            dma((15,)),
-            dma((16,)),
+            dma((BATCHES - DIRECT, 15)),
+            dma((BATCHES - DIRECT, 16)),
             dma((BATCHES,)),
             dma((BATCHES,)),
             dma((4,)),

time: 63.3 us -> 60.3 us (0.953)
  Pallas kernels: 60.5 us -> 57.9 us
    pallas_call x1, Pallas kernels: 60.5 us -> 57.9 us  [local(): pl.pallas_call(functools.partial(kernel, seq_len), out_shape=(jax.ShapeDt...]
where the time goes in v3:
time: 60.3 us; the launch traced here: 60 us
  Pallas kernels  57.9 us (96%)
  local copies, waits for them, and re-layouts  1.48 us (2%)
  between operations  0.64 us (1%)
    pallas_call x1, Pallas kernels, local(): pl.pallas_call(functools.partial(kernel, seq_len), out_shape=(jax.ShapeDt...  57.9 us
    unnamed x2, local copies, waits for them, and re-layouts  1.48 us

profile of v3, /device:TPU:25, one launch (start us, length us, event | category | flops | bytes accessed | tf_op | source)
XLA Modules:
  0.0 60.0 jit_solution(10260549863297122229)
XLA Ops:
  0.6 57.9 %step.1 = (bf16[1,128,4096]{2,1,0:T(8,128)(2,1)S(1)}, f32[1,128]{1,0:T(1,128)S(1)}) custom-call(bf16[1,128,4096]{2,1,0:T(8,128)(2,1)} %x_hbm.1, s32[1,128]{1,0:T(1,128)} %pos_hbm.1, bf16[1,128,4096]{2,1,0:T(8,128)(2,1)} %teach_hbm.1, bf16[1,2,128,128]{3,2,1,0:T(8,128)(2,1)} %gw_hbm.1, f32[2,4096]{1,0:T(2,128)} %gb_hbm.1, f32[4,4096]{1,0:T(4,128)} %cw_hbm.1, ...), custom_call_target="tpu_custom_call" | custom-call | tf_op jit(solution)/shard_map/step/pallas_call | solution.py:553
  58.5 1.0 %copy.12 = bf16[1,128,4096]{2,1,0:T(8,128)(2,1)} copy(bf16[1,128,4096]{2,1,0:T(8,128)(2,1)S(1)} %get-tuple-element.4) | data formatting | bytes 2097152
  59.5 0.5 copy.13

commit v4 on v3

--- a/solution.py
+++ b/solution.py
@@ -11,9 +11,8 @@
 MESH = pl.DeviceIdType.MESH
 F32 = jnp.float32
 BF16 = jnp.bfloat16
-SIZES = (1, 2, 2, 2, 1)
-BATCHES = len(SIZES)
-LAST = BATCHES - 1
+HEADS_IN = (5, 8, 8, 8, 3)
+BATCHES = len(HEADS_IN)
 DIRECT = 3
 
 
@@ -116,10 +115,7 @@
 
     partner = (1 - g, z, s)
     other_core = in_row(here // 2 * 2 + 1 - core)
-    greeted = [at_z(dz) for dz in (8, -8, 4, -4)]
-    for dz in (2, -2, 1, -1):
-        for d in range(4):
-            greeted.append(at_z(dz)[:2] + (row * 8 + lax.rem(xc + d, 4) * 2 + core,))
+    greeted = [at_z(dz) for dz in (8, -8, 4, -4, 3, -3, 2, -2, 1, -1)]
     greeted += [partner] + [(g, z, lax.rem(s + d, places)) for d in range(1, 16)]
     barrier = pltpu.get_barrier_semaphore()
     for device in greeted:
@@ -130,50 +126,62 @@
     blocks = [pl.ds(32 * k, 32) for k in range(4)]
     quarter = pl.ds(pl.multiple_of(xc * 32, 32), 32)
 
-    def first(j, kind):
-        return 8 * j + kind * SIZES[j]
+    def span(j, kind):
+        if j == 0:
+            return kind, 2 if kind == 3 else 1
+        return (32 + kind, 1) if j == 4 else (8 * j + 2 * kind, 2)
+
+    def kinds(j, by_relay):
+        if not by_relay:
+            return (1, 2)
+        return {0: (3,), 4: (0,)}.get(j, (0, 3))
 
     def piece(u, count):
         return wbuf.at[pl.ds(u, count), :, quarter, :]
 
     def far_copy(j, down):
-        source = (8 * 2 + (1 if down else 0)) if j > 2 else 0
-        target = 8 * j + (1 if down and j < 4 else 0)
-        k = j - 1 + (4 if down else 0)
-        dz = 4 if j % 2 else 8
-        return remote(piece(source, 1), piece(target, 1), far_s.at[k], far_r.at[k], at_z(-dz if down else dz))
+        side = 1 if down else 0
+        k = j - 1 + 4 * side
+        dz = (4 if j % 2 else 8) * (-1 if down else 1)
+        if j == 4:
+            gate = pl.ds(side, 1)
+            src, dst = (wbuf.at[pl.ds(u, 1), gate, quarter, :] for u in (16 + side, 32))
+        else:
+            src, dst = piece(16 + side if j == 3 else 0, 1), piece(8 * j + side, 1)
+        return remote(src, dst, far_s.at[k], far_r.at[k], at_z(dz))
 
     def send_near(j):
-        count = SIZES[j]
-        src = piece(first(j, 0), count)
-        for d in (2, 1, 3, 0) if j == LAST else (0,):
-            place = row * 8 + lax.rem(xc + d, 4) * 2 + core
-            for kind, dz in ((3, 2), (1, 1), (2, -1)):
-                dst = piece(first(j, kind), count)
-                to = (g, lax.rem(z + dz + planes, planes), place)
-                remote(src, dst, near_s.at[j], near_r.at[kind, j], to).start()
+        def send(u, count, kind, skip, dz, group=j):
+            dst = piece(span(group, kind)[0] + skip, count)
+            remote(piece(u, count), dst, near_s.at[j], near_r.at[kind, group], at_z(dz)).start()
+
+        u, count = span(j, 0)
+        above = u + count - 1
+        if j == 3:
+            send(above, 1, 1, 0, -3, 4)
+            send(u, 1, 2, 0, 3, 4)
+        send(u, 1, 3, 0, 2)
+        send(above, 1, 3, 1, -2)
+        send(u, count, 1, 0, 1)
+        send(u, count, 2, 0, -1)
+
+    def near_sent(j):
+        return {0: wbuf.at[pl.ds(0, 1)], 3: wbuf.at[pl.ds(0, 2)]}.get(j, three(j, 0))
 
     def wait_near(j, kind):
-        dst = piece(first(j, kind), SIZES[j])
-        await_bytes(dst, near_r.at[kind, j])
+        await_bytes(piece(*span(j, kind)), near_r.at[kind, j])
 
     def send_x(j, kind):
-        src = piece(first(j, kind), SIZES[j])
-        for d in (1, 3, 2):
+        src = piece(*span(j, kind))
+        for d in (2, 1, 3):
             to = in_row(lax.rem(xc + d, 4) * 2 + core)
             remote(src, src, x_s.at[kind, j], x_r.at[kind, j], to).start()
 
     def three(j, kind):
-        return wbuf.at[pl.ds(first(j, kind), SIZES[j]), :, pl.ds(0, 96), :]
-
-    def await_x(j, kind):
-        if j == LAST and kind:
-            await_bytes(wbuf.at[pl.ds(first(j, kind), 1)], near_r.at[kind, j])
-        else:
-            await_bytes(three(j, kind), x_r.at[kind, j])
+        return wbuf.at[pl.ds(*span(j, kind)), :, pl.ds(0, 96), :]
 
     def chip_copy(j, kind):
-        src = wbuf.at[pl.ds(first(j, kind), SIZES[j])]
+        src = wbuf.at[pl.ds(*span(j, kind))]
         return remote(src, src, chip_s.at[kind, j], chip_r.at[kind, j], other_core)
 
     def both(for_relay, for_other):
@@ -186,7 +194,7 @@
             for_other()
 
     def far_copies(j):
-        return [far_copy(j, down) for down in ((False, True) if j < 4 else (True,))]
+        return [far_copy(j, down) for down in (False, True)]
 
     def start_far(j):
         for copy in far_copies(j):
@@ -200,47 +208,33 @@
             if j == 2:
                 start_far(4)
                 start_far(3)
-            send_near(j)
+            if j < 4:
+                send_near(j)
             send_x(j, 0)
 
     def step_near(j):
-        if j == LAST:
-            return
-
-        def for_relay():
-            wait_near(j, 3)
-            send_x(j, 3)
-
-        def for_other():
-            for kind in (1, 2):
-                wait_near(j, kind)
-                send_x(j, kind)
-
-        both(for_relay, for_other)
+        def get(by_relay):
+            for kind in kinds(j, by_relay):
+                if kind:
+                    wait_near(j, kind)
+                    send_x(j, kind)
+
+        both(functools.partial(get, True), functools.partial(get, False))
 
     def step_x(j):
-        def for_relay():
-            for kind in (0, 3) if j else (3,):
-                await_x(j, kind)
+        def hand_over(by_relay):
+            for kind in kinds(j, by_relay):
+                await_bytes(three(j, kind), x_r.at[kind, j])
                 chip_copy(j, kind).start()
 
-        def for_other():
-            for kind in (1, 2):
-                await_x(j, kind)
-                chip_copy(j, kind).start()
-
-        both(for_relay, for_other)
+        both(functools.partial(hand_over, True), functools.partial(hand_over, False))
 
     def step_chip(j):
-        def for_relay():
-            for kind in (1, 2):
+        def get(by_relay):
+            for kind in kinds(j, not by_relay):
                 chip_copy(j, kind).wait_recv()
 
-        def for_other():
-            for kind in (0, 3) if j else (3,):
-                chip_copy(j, kind).wait_recv()
-
-        both(for_relay, for_other)
+        both(functools.partial(get, True), functools.partial(get, False))
 
     @pl.when(relay)
     def _():
@@ -300,10 +294,16 @@
         return 0
 
     def head_of(j, index):
-        count = SIZES[j]
-        kind, side = index // count, index % count
-        ahead = jnp.where(kind == 0, 0, jnp.where(kind == 1, -1, jnp.where(kind == 2, 1, -2)))
-        return lax.rem(z + ahead + jnp.where(side == 0, -4 * j, 4 * j) + 2 * planes, planes)
+        if j in (0, 4):
+            away = jnp.int32(0)
+            for k, dz in enumerate((0, -1, 1, -2, 2) if j == 0 else (16, 15, -15)):
+                away = jnp.where(index == k, dz, away)
+        else:
+            kind, side = index // 2, index % 2
+            side = 2 * side - 1
+            near = jnp.where(kind == 0, 0, jnp.where(kind == 1, -1, jnp.where(kind == 2, 1, 2 * side)))
+            away = near + 4 * j * side
+        return lax.rem(z + away + planes, planes)
 
     sub = lax.broadcasted_iota(jnp.int32, (8, HS), 0)
 
@@ -345,7 +345,8 @@
         return 0
 
     def compute(j):
-        lax.fori_loop(0, 4 * SIZES[j], functools.partial(gates, j), 0, unroll=4)
+        unroll = HEADS_IN[j] if HEADS_IN[j] < 8 else 4
+        lax.fori_loop(0, HEADS_IN[j], functools.partial(gates, j), 0, unroll=unroll)
 
     def mine(j):
         return pl.ds(8 * j, 8)
@@ -431,34 +432,29 @@
             acc_b[...] += wide * wide
             return 0
 
-        lax.fori_loop(0, 4 * SIZES[j], finish, 0, unroll=4)
+        unroll = HEADS_IN[j] if HEADS_IN[j] < 8 else 4
+        lax.fori_loop(0, HEADS_IN[j], finish, 0, unroll=unroll)
 
     def sent(j):
-        def by_relay():
-            if j:
+        def clear(by_relay):
+            if by_relay and j:
                 for copy in far_copies(j):
                     copy.wait_send()
-            await_bytes(wbuf.at[pl.ds(0, 3)] if j == LAST else three(j, 0), near_s.at[j])
-            for kind in (0, 3) if j else (3,):
-                if j < LAST or kind == 0:
-                    await_bytes(three(j, kind), x_s.at[kind, j])
+            if by_relay and j < 4:
+                await_bytes(near_sent(j), near_s.at[j])
+            for kind in kinds(j, by_relay):
+                await_bytes(three(j, kind), x_s.at[kind, j])
                 chip_copy(j, kind).wait_send()
 
-        def by_other():
-            for kind in (1, 2):
-                if j < LAST:
-                    await_bytes(three(j, kind), x_s.at[kind, j])
-                chip_copy(j, kind).wait_send()
-
-        both(by_relay, by_other)
+        both(functools.partial(clear, True), functools.partial(clear, False))
 
     heads = x_v.shape[1] // HS
     lax.fori_loop(0, heads // 2, conv_head, 0, unroll=4)
     step_near(0)
     step_far(1)
+    step_far(2)
     lax.fori_loop(heads // 2, heads, conv_head, 0, unroll=4)
     step_x(0)
-    step_far(2)
     step_near(1)
     step_chip(0)
     compute(0)
@@ -469,10 +465,11 @@
     step_chip(1)
     compute(1)
     send_row(1)
+    step_row(0)
+    step_far(4)
     step_x(2)
-    step_far(4)
     step_near(3)
-    step_row(0)
+    step_near(4)
     step_chip(2)
     compute(2)
     send_row(2)

time: 60.3 us -> 58.3 us (0.967)
  Pallas kernels: 57.9 us -> 55.8 us
    pallas_call x1, Pallas kernels: 57.9 us -> 55.8 us  [local(): pl.pallas_call(functools.partial(kernel, seq_len), out_shape=(jax.ShapeDt...]
where the time goes in v4:
time: 58.3 us; the launch traced here: 57.9 us
  Pallas kernels  55.8 us (96%)
  local copies, waits for them, and re-layouts  1.48 us (3%)
  between operations  0.64 us (1%)
    pallas_call x1, Pallas kernels, local(): pl.pallas_call(functools.partial(kernel, seq_len), out_shape=(jax.ShapeDt...  55.8 us
    unnamed x2, local copies, waits for them, and re-layouts  1.48 us

profile of v4, /device:TPU:25, one launch (start us, length us, event | category | flops | bytes accessed | tf_op | source)
XLA Modules:
  0.0 57.9 jit_solution(6328364690911489146)
XLA Ops:
  0.6 55.8 %step.1 = (bf16[1,128,4096]{2,1,0:T(8,128)(2,1)S(1)}, f32[1,128]{1,0:T(1,128)S(1)}) custom-call(bf16[1,128,4096]{2,1,0:T(8,128)(2,1)} %x_hbm.1, s32[1,128]{1,0:T(1,128)} %pos_hbm.1, bf16[1,128,4096]{2,1,0:T(8,128)(2,1)} %teach_hbm.1, bf16[1,2,128,128]{3,2,1,0:T(8,128)(2,1)} %gw_hbm.1, f32[2,4096]{1,0:T(2,128)} %gb_hbm.1, f32[4,4096]{1,0:T(4,128)} %cw_hbm.1, ...), custom_call_target="tpu_custom_call" | custom-call | tf_op jit(solution)/shard_map/step/pallas_call | solution.py:550
  56.4 1.0 %copy.12 = bf16[1,128,4096]{2,1,0:T(8,128)(2,1)} copy(bf16[1,128,4096]{2,1,0:T(8,128)(2,1)S(1)} %get-tuple-element.4) | data formatting | bytes 2097152
  57.4 0.5 copy.13

commit v5 on v4

--- a/solution.py
+++ b/solution.py
@@ -35,8 +35,9 @@
     cw_hbm,
     cb_hbm,
     rate_hbm,
-    out_hbm,
-    loss_ref,
+    student,
+    tbuf,
+    norm_ref,
     x_v,
     halo,
     pos_v,
@@ -44,7 +45,6 @@
     cw_v,
     cb_v,
     rate_v,
-    tbuf,
     wbuf,
     convb,
     prod_b,
@@ -59,9 +59,7 @@
     masks,
     tmp,
     acc_b,
-    student,
     load_sem,
-    out_sem,
     far_s,
     far_r,
     near_s,
@@ -491,21 +489,10 @@
     step_direct(3)
     step_direct(4)
 
-    out_copy = pltpu.make_async_copy(student, out_hbm.at[0], out_sem)
-    out_copy.start()
-    width = x_v.shape[1]
-    mean_sq = jnp.sum(acc_b[...], axis=1, keepdims=True) * (1.0 / width)
-    tmp[...] = jnp.broadcast_to(lax.rsqrt(mean_sq + 1e-06), (HS, HS))
-    for k, block in enumerate(blocks):
-        teacher_copies[k].wait_recv()
-
-        def loss_head(head, total):
-            cols = columns(head)
-            diff = student[block, cols].astype(F32) * tmp[block, :] - tbuf[block, cols].astype(F32)
-            return total + diff * diff
-
-        acc_b[block, :] = lax.fori_loop(0, heads, loss_head, jnp.zeros((32, HS), F32), unroll=4)
-    loss_ref[...] = jnp.sum(jnp.transpose(acc_b[...]), axis=0, keepdims=True) * (1.0 / width)
+    mean_sq = jnp.sum(acc_b[...], axis=1, keepdims=True) * (1.0 / x_v.shape[1])
+    norm_ref[...] = jnp.broadcast_to(lax.rsqrt(mean_sq + 1e-06), (HS, HS))
+    for copy in teacher_copies:
+        copy.wait_recv()
 
     for copy in teacher_copies:
         copy.wait_send()
@@ -528,6 +515,22 @@
             for j in range(DIRECT, BATCHES):
                 direct_copy(j, d).wait_send()
 
+
+def finish_kernel(student, target, norm_ref, out_hbm, loss_ref, acc_b, out_sem):
+    out_copy = pltpu.make_async_copy(student, out_hbm.at[0], out_sem)
+    out_copy.start()
+    width = student.shape[1]
+    for k in range(4):
+        block = pl.ds(32 * k, 32)
+
+        def loss_head(head, total):
+            cols = pl.ds(pl.multiple_of(head * HS, HS), HS)
+            diff = student[block, cols].astype(F32) * norm_ref[block, :] - target[block, cols].astype(F32)
+            return total + diff * diff
+
+        zero = jnp.zeros((32, HS), F32)
+        acc_b[block, :] = lax.fori_loop(0, width // HS, loss_head, zero, unroll=8)
+    loss_ref[...] = jnp.sum(jnp.transpose(acc_b[...]), axis=0, keepdims=True) * (1.0 / width)
     out_copy.wait()
 
 
@@ -547,14 +550,15 @@
         decay_rate.reshape(1, width),
     )
     operands = [pltpu.with_memory_space_constraint(v, pltpu.HBM) for v in operands]
-    out, loss = pl.pallas_call(
+    held = pl.pallas_call(
         functools.partial(kernel, seq_len),
         out_shape=(
-            jax.ShapeDtypeStruct((1, rows, width), BF16),
-            jax.ShapeDtypeStruct((1, rows), F32),
+            jax.ShapeDtypeStruct((rows, width), BF16),
+            jax.ShapeDtypeStruct((rows, width), BF16),
+            jax.ShapeDtypeStruct((rows, HS), F32),
         ),
         in_specs=[pl.BlockSpec(memory_space=pltpu.HBM)] * 8,
-        out_specs=(pl.BlockSpec(memory_space=pltpu.HBM), pl.BlockSpec(memory_space=pltpu.VMEM)),
+        out_specs=[pl.BlockSpec(memory_space=pltpu.VMEM)] * 3,
         scratch_shapes=[
             pltpu.VMEM((rows, width), BF16),
             pltpu.VMEM((16, width), BF16),
@@ -563,7 +567,6 @@
             pltpu.VMEM((4, width), F32),
             pltpu.VMEM((1, width), F32),
             pltpu.VMEM((1, width), F32),
-            pltpu.VMEM((rows, width), BF16),
             pltpu.VMEM((slots, 2, HS, HS), BF16),
             pltpu.VMEM((width // HS, rows, HS), BF16),
             pltpu.VMEM((slots, rows, HS), F32),
@@ -578,9 +581,7 @@
             pltpu.VMEM((3, rows, HS), F32),
             pltpu.VMEM((rows, HS), F32),
             pltpu.VMEM((rows, HS), F32),
-            pltpu.VMEM((rows, width), BF16),
             dma((7,)),
-            dma,
             dma((8,)),
             dma((8,)),
             dma((BATCHES,)),
@@ -605,7 +606,18 @@
         ),
         name="step",
     )(*operands)
-    return out, loss
+    return pl.pallas_call(
+        finish_kernel,
+        out_shape=(
+            jax.ShapeDtypeStruct((1, rows, width), BF16),
+            jax.ShapeDtypeStruct((1, rows), F32),
+        ),
+        in_specs=[pl.BlockSpec(memory_space=pltpu.VMEM)] * 3,
+        out_specs=(pl.BlockSpec(memory_space=pl.ANY), pl.BlockSpec(memory_space=pltpu.VMEM)),
+        scratch_shapes=[pltpu.VMEM((rows, HS), F32), dma],
+        compiler_params=pltpu.CompilerParams(vmem_limit_bytes=16 << 20),
+        name="loss",
+    )(*held)
 
 
 def solution(mesh):

time: 58.3 us -> 57.4 us (0.985)
  local copies, waits for them, and re-layouts: 1.48 us -> 0 us
    pallas_call x0 -> x1, Pallas kernels: none -> 1.49 us  [local(): pl.pallas_call(finish_kernel, out_shape=(jax.ShapeDtypeStruct((1, rows, w...]
    unnamed x2 -> x0, local copies, waits for them, and re-layouts: 1.48 us -> none
    pallas_call x1, Pallas kernels: 55.8 us -> 54.8 us  [local(): pl.pallas_call(functools.partial(kernel, seq_len), out_shape=(jax.ShapeDt...]
where the time goes in v5:
time: 57.4 us; the launch traced here: 57 us
  Pallas kernels  56.3 us (98%)
  between operations  0.64 us (1%)
    pallas_call x1, Pallas kernels, local(): pl.pallas_call(functools.partial(kernel, seq_len), out_shape=(jax.ShapeDt...  54.8 us
    pallas_call x1, Pallas kernels, local(): pl.pallas_call(finish_kernel, out_shape=(jax.ShapeDtypeStruct((1, rows, w...  1.49 us

profile of v5, /device:TPU:25, one launch (start us, length us, event | category | flops | bytes accessed | tf_op | source)
XLA Modules:
  0.0 57.0 jit_solution(11894062305423581749)
XLA Ops:
  0.6 54.8 %step.1 = (bf16[128,4096]{1,0:T(8,128)(2,1)S(1)}, bf16[128,4096]{1,0:T(8,128)(2,1)S(1)}, f32[128,128]{1,0:T(8,128)S(1)}) custom-call(bf16[1,128,4096]{2,1,0:T(8,128)(2,1)} %x_hbm.1, s32[1,128]{1,0:T(1,128)} %pos_hbm.1, bf16[1,128,4096]{2,1,0:T(8,128)(2,1)} %teach_hbm.1, bf16[1,2,128,128]{3,2,1,0:T(8,128)(2,1)} %gw_hbm.1, f32[2,4096]{1,0:T(2,128)} %gb_hbm.1, ...), custom_call_target="tpu_custom_call" | custom-call | tf_op jit(solution)/shard_map/step/pallas_call | solution.py:553
  55.5 1.5 %loss.1 = (bf16[1,128,4096]{2,1,0:T(8,128)(2,1)}, f32[1,128]{1,0:T(1,128)}) custom-call(bf16[128,4096]{1,0:T(8,128)(2,1)S(1)} %get-tuple-element.5.student, bf16[128,4096]{1,0:T(8,128)(2,1)S(1)} %get-tuple-element.6.target, f32[128,128]{1,0:T(8,128)S(1)} %get-tuple-element.7.norm_ref), custom_call_target="tpu_custom_call" | custom-call | tf_op jit(solution)/shard_map/loss/pallas_call | solution.py:609

commit v6 on v5

--- a/solution.py
+++ b/solution.py
@@ -478,10 +478,10 @@
     step_chip(3)
     compute(3)
     send_direct(3)
-    step_row(2)
     step_chip(4)
     compute(4)
     send_direct(4)
+    step_row(2)
     step_y(1)
     for j in range(BATCHES):
         sent(j)

time: 57.4 us -> 57.9 us (level)
  Pallas kernels: 56.3 us -> 57.1 us
    pallas_call x1, Pallas kernels: 54.8 us -> 55.6 us  [local(): pl.pallas_call(functools.partial(kernel, seq_len), out_shape=(jax.ShapeDt...]
where the time goes in v6:
time: 57.9 us; the launch traced here: 57.8 us
  Pallas kernels  57.1 us (99%)
  between operations  0.64 us (1%)
    pallas_call x1, Pallas kernels, local(): pl.pallas_call(functools.partial(kernel, seq_len), out_shape=(jax.ShapeDt...  55.6 us
    pallas_call x1, Pallas kernels, local(): pl.pallas_call(finish_kernel, out_shape=(jax.ShapeDtypeStruct((1, rows, w...  1.49 us

profile of v6, /device:TPU:25, one launch (start us, length us, event | category | flops | bytes accessed | tf_op | source)
XLA Modules:
  0.0 57.8 jit_solution(14424779792327611347)
XLA Ops:
  0.6 55.6 %step.1 = (bf16[128,4096]{1,0:T(8,128)(2,1)S(1)}, bf16[128,4096]{1,0:T(8,128)(2,1)S(1)}, f32[128,128]{1,0:T(8,128)S(1)}) custom-call(bf16[1,128,4096]{2,1,0:T(8,128)(2,1)} %x_hbm.1, s32[1,128]{1,0:T(1,128)} %pos_hbm.1, bf16[1,128,4096]{2,1,0:T(8,128)(2,1)} %teach_hbm.1, bf16[1,2,128,128]{3,2,1,0:T(8,128)(2,1)} %gw_hbm.1, f32[2,4096]{1,0:T(2,128)} %gb_hbm.1, ...), custom_call_target="tpu_custom_call" | custom-call | tf_op jit(solution)/shard_map/step/pallas_call | solution.py:553
  56.3 1.5 %loss.1 = (bf16[1,128,4096]{2,1,0:T(8,128)(2,1)}, f32[1,128]{1,0:T(1,128)}) custom-call(bf16[128,4096]{1,0:T(8,128)(2,1)S(1)} %get-tuple-element.5.student, bf16[128,4096]{1,0:T(8,128)(2,1)S(1)} %get-tuple-element.6.target, f32[128,128]{1,0:T(8,128)S(1)} %get-tuple-element.7.norm_ref), custom_call_target="tpu_custom_call" | custom-call | tf_op jit(solution)/shard_map/loss/pallas_call | solution.py:609
